TPU v7x, 32 devices: a whole 2x2x4 slice. The times are simulated.
32 devices in a mesh: mem: 4 (over y, core), lat: 2 (over x), lon: 4 (over z).
Axes of the slice: x: 2, y: 2, z: 4, core: 2. Of those that a mesh axis runs over, the one named last changes fastest.
Arguments:
- perturbations: bfloat16 [8, 4, 768, 1536], P('mem', None, 'lat', 'lon'), may hold values from -2 to 2
- innovation: float32 [2, 8192], P('lat', 'lon'), may hold values from -4.2 to 4.2
- obs_weight: float32 [2, 8192], P('lat', 'lon'), may hold values from 0.5 to 6, as said below
- obs_cell: int32 [2, 8192], P('lat', 'lon'), may hold values from 0 to 147455
- obs_level: int32 [2, 8192], P('lat', 'lon'), may hold values from 0 to 3
- cutoff: int32 [4], replicated, may hold values from 16 to 127
Outputs:
- solution: float32 [8, 4, 768, 512], P('mem', None, ('lat', 'lon'))
- residual: float32 [8, 4, 768, 512], P('mem', None, ('lat', 'lon'))
Inputs may be any that keep to these rules, and one draw needn't show every extreme that they name: `obs_weight`: positive weights.
All inputs are finite; a program needn't handle non-finite values.
Results may differ from a plain program's by a relative error of at most 0.0008.
Values may be sent and summed in bfloat16 or wider, within the bound.
No kernel may reach another device: no remote copies, remote signals or barrier semaphores. Data moves between devices by JAX's collectives and lax.ppermute only.
A program may use at most 64 MiB of HBM per device.

v0:
```python
import jax
import jax.numpy as jnp
from jax import lax
from jax.sharding import PartitionSpec as P

NLON = 1536
KMAX = 256
ITERS = 2


def basis_table(transposed):
    factor = 2.0 * jnp.pi / NLON
    if transposed:
        columns = jnp.arange(NLON, dtype=jnp.int32)[None, :]
        cos_waves = jnp.arange(KMAX, dtype=jnp.int32)[:, None]
        axis_join = 0
    else:
        columns = jnp.arange(NLON, dtype=jnp.int32)[:, None]
        cos_waves = jnp.arange(KMAX, dtype=jnp.int32)[None, :]
        axis_join = 1
    cos_phase = (columns * cos_waves % NLON).astype(jnp.float32) * factor
    sin_phase = (columns * (cos_waves + 1) % NLON).astype(jnp.float32) * factor
    joined = jnp.concatenate([jnp.cos(cos_phase), jnp.sin(sin_phase)], axis=axis_join)
    return joined / jnp.sqrt(jnp.float32(KMAX))


def spectrum_of(cutoff):
    wavenumbers = jnp.concatenate(
        [jnp.arange(KMAX, dtype=jnp.float32), jnp.arange(1, KMAX + 1, dtype=jnp.float32)]
    )
    scaled = wavenumbers[None, :] / cutoff.astype(jnp.float32)[:, None]
    return 1.0 / (1.0 + scaled * scaled)


def member_total(partial_value):
    return lax.psum(partial_value, "mem")


def norm_total(residual):
    return lax.psum(jnp.sum(residual * residual), ("mem", "lat", "lon"))


def body(perturbations, innovation, obs_weight, obs_cell, obs_level, cutoff):
    members_here, levels, tile_rows, tile_cols = perturbations.shape
    line_rows = tile_rows // lax.axis_size("lon")
    basis_rows = basis_table(False)
    basis_cols = basis_table(True)
    spectrum = spectrum_of(cutoff)
    located = (obs_level * (tile_rows * tile_cols) + obs_cell).reshape(-1)
    weights = obs_weight.reshape(-1)

    def gridded_of(weighted):
        field = jnp.zeros((levels * tile_rows * tile_cols,), jnp.float32).at[located].add(weighted)
        return field.reshape(levels, tile_rows, tile_cols)

    def analyse(products):
        summed = jnp.dot(
            products.reshape(-1, NLON),
            basis_rows,
            precision=lax.Precision.HIGHEST,
            preferred_element_type=jnp.float32,
        )
        return (
            summed.reshape(members_here, levels, line_rows, 2 * KMAX) * spectrum[None, :, None, :]
        )

    line_pert = lax.all_to_all(perturbations, "lon", split_axis=2, concat_axis=3, tiled=True)

    def adjoint_part(gridded):
        grid_lines = lax.all_to_all(gridded, "lon", split_axis=1, concat_axis=2, tiled=True)
        products = line_pert.astype(jnp.float32) * grid_lines[None]
        return analyse(products)

    right_side = adjoint_part(gridded_of(weights * innovation.reshape(-1)))
    solution = jnp.zeros_like(right_side)
    residual = right_side
    direction = right_side
    norm_now = norm_total(residual)
    for iteration in range(ITERS):
        coeffs = direction * spectrum[None, :, None, :]
        synthesized = jnp.dot(
            coeffs.reshape(-1, 2 * KMAX),
            basis_cols,
            precision=lax.Precision.HIGHEST,
            preferred_element_type=jnp.float32,
        )
        forward_synthesized = synthesized.reshape(members_here, levels, line_rows, NLON)
        partial_value = jnp.sum(line_pert.astype(jnp.float32) * forward_synthesized, axis=0)
        on_tiles = lax.all_to_all(partial_value, "lon", split_axis=2, concat_axis=1, tiled=True)
        increment = member_total(on_tiles)
        sampled = increment.reshape(-1)[located]
        image = direction + adjoint_part(gridded_of(weights * sampled))
        curvature = lax.psum(jnp.sum(direction * image), ("mem", "lat", "lon"))
        step_size = norm_now / curvature
        solution = solution + step_size * direction
        residual = residual - step_size * image
        if iteration + 1 < ITERS:
            norm_next = norm_total(residual)
            direction = residual + norm_next / norm_now * direction
            norm_now = norm_next
    return (solution, residual)


def solution(mesh):
    placed = (
        P("mem", None, "lat", "lon"),
        P("lat", "lon"),
        P("lat", "lon"),
        P("lat", "lon"),
        P("lat", "lon"),
        P(),
    )
    return jax.shard_map(
        body,
        mesh=mesh,
        in_specs=placed,
        out_specs=(P("mem", None, ("lat", "lon"), None), P("mem", None, ("lat", "lon"), None)),
        check_vma=False,
    )
```

profile of v0, /device:TPU:0, one launch (start us, length us, event | category | flops | bytes accessed | tf_op | source)
XLA Modules:
  0.0 842.8 jit_solution(17484831876931123835)
XLA Ops:
  8.6 12.8 %scatter_custom_fusion = f32[589824]{0:T(1024)} fusion(s32[2048]{0:T(1024)S(1)} %bitcast.74, f32[2048]{0:T(1024)S(1)} %mul.200, f32[]{:T(128)} %constant.20.clone.1), kind=kCustom, calls=%fused_computation.75 | custom fusion | flops 2048 | bytes 2359300 | tf_op jit(solution)/shard_map/scatter-add | solution.py:53
  21.4 3.4 reshape.134
  24.8 4.6 copy.45
  29.4 6.3 all-to-all-start.1
  35.7 4.9 copy.43
  40.6 49.0 %all-to-all-done.1 = f32[4,384,384]{2,0,1:T(4,128)} async-done(((f32[4,384,384]{2,0,1:T(4,128)}), f32[4,384,384]{2,0,1:T(4,128)}, u32[]{:S(2)}, u32[]{:S(2)}) %all-to-all-start.1) | async-done | bytes 2359328 | tf_op jit(solution)/shard_map/all_to_all | solution.py:70
  89.6 4.5 all-to-all-start
  94.5 5.9 fusion.18
  100.4 8.1 fusion.24
  108.5 6.8 fusion.21
  115.3 7.0 fusion.27
  122.3 1.8 copy.46
  124.2 1.8 copy.66
  125.9 21.6 %all-to-all-done = bf16[2,4,384,384]{3,1,0,2:T(4,128)(2,1)} async-done(((bf16[2,4,384,384]{3,1,0,2:T(4,128)(2,1)}), bf16[2,4,384,384]{3,1,0,2:T(4,128)(2,1)}, u32[]{:S(2)}, u32[]{:S(2)}) %all-to-all-start) | async-done | bytes 2359328 | tf_op jit(solution)/shard_map/all_to_all | solution.py:67
  147.6 5.7 copy.70
  153.3 6.4 reshape.141
  159.6 10.9 %fusion.47 = f32[2,4,96,512]{3,2,1,0:T(8,128)S(1)} fusion(f32[1536,256]{1,0:T(8,128)} %fusion.21, f32[1536,256]{1,0:T(8,128)S(1)} %fusion.18, f32[2,4,96,1536]{3,2,1,0:T(8,128)} %reshape.141, f32[4,96,1536]{2,1,0:T(8,128)} %bitcast.63, f32[4,512]{1,0:T(4,128)S(1)} %fusion.65), kind=kOutput, calls=%fused_computation.70 | convolution fusion | flops 7250903040 | bytes 11804672 | tf_op jit(solution)/shard_map/dot_general | solution.py:57
  170.6 10.3 %multiply_reduce_fusion.1 = f32[4,96,1536]{2,1,0:T(8,128)} fusion(f32[2,4,96,1536]{3,2,1,0:T(8,128)S(1)} %copy-done, f32[256,1536]{1,0:T(8,128)S(1)} %copy-done.10, f32[256,1536]{1,0:T(8,128)S(1)} %copy-done.8, f32[2,4,96,512]{3,2,1,0:T(8,128)S(1)} %fusion.47, f32[4,512]{1,0:T(4,128)S(1)} %fusion.65), kind=kOutput, calls=%fused_computation.11 | convolution fusion | flops 7251492864 | bytes 11804672 | tf_op jit(solution)/shard_map/dot_general | solution.py:81
  180.9 4.5 copy.48
  185.4 75.5 %all_to_all.90 = f32[4,96,1536]{1,0,2:T(4,128)} all-to-all(f32[4,96,1536]{1,0,2:T(4,128)} %copy.48), channel_id=1, replica_groups=mesh['mem'=4,'lat'=2,'lon'=4] {'lon'}, dimensions={2} | all-to-all | bytes 4718592 | tf_op jit(solution)/shard_map/all_to_all | solution.py:89
  261.0 4.7 copy.50
  265.6 3.2 reshape.135
  269.0 54.8 %all-reduce.4.cloned.1.call-done = f32[589824]{0:T(1024)} async-done(((f32[589824]{0:T(1024)}), f32[589824]{0:T(1024)}) %all-reduce.4.cloned.1.call-update) | async-done | bytes 2359312 | tf_op jit(solution)/shard_map/psum | solution.py:36
  323.8 24.5 %gather_fusion = f32[2048]{0:T(1024)S(1)} fusion(f32[589824]{0:T(1024)} %all-reduce.4.cloned.1.call-done, s32[2048]{0:T(1024)S(1)} %broadcast_clamp_fusion), kind=kCustom, calls=%fused_computation | custom fusion | bytes 24576 | tf_op jit(solution)/shard_map/gather | solution.py:91
  348.3 12.8 %scatter_custom_fusion.1 = f32[589824]{0:T(1024)} fusion(s32[2048]{0:T(1024)S(1)} %bitcast.76, f32[2048]{0:T(1024)S(1)} %mul.226, f32[]{:T(128)} %constant.20.clone.1), kind=kCustom, calls=%fused_computation.73 | custom fusion | flops 2048 | bytes 2359300 | tf_op jit(solution)/shard_map/scatter-add | solution.py:53
  361.1 3.4 reshape.136
  364.5 3.2 copy.51
  367.7 58.7 %all_to_all.91 = f32[4,384,384]{2,0,1:T(4,128)S(1)} all-to-all(f32[4,384,384]{2,0,1:T(4,128)S(1)} %copy.51), channel_id=1, replica_groups=mesh['mem'=4,'lat'=2,'lon'=4] {'lon'}, dimensions={1} | all-to-all | bytes 4718592 | tf_op jit(solution)/shard_map/all_to_all | solution.py:70
  428.5 8.6 %multiply_reduce_fusion.4 = (f32[]{:T(128)}, f32[]{:T(128)}, f32[2,4,96,512]{3,2,1,0:T(8,128)S(1)}) fusion(f32[2,4,96,512]{3,2,1,0:T(8,128)S(1)} %fusion.47, f32[4,512]{1,0:T(4,128)S(1)} %fusion.65, f32[1536,256]{1,0:T(8,128)S(1)} %copy-done.4, f32[1536,256]{1,0:T(8,128)S(1)} %copy-done.2, f32[2,4,96,1536]{3,2,1,0:T(8,128)S(1)} %bitcast.59, ...), kind=kOutput, calls=%fused_computation.45 | convolution fusion | flops 7252869120 | bytes 13377544 | tf_op jit(solution)/shard_map/dot_general | solution.py:57
  437.1 38.3 %all-reduce = (f32[]{:T(128)}, f32[]{:T(128)}) all-reduce(f32[]{:T(128)} %get-tuple-element.3, f32[]{:T(128)} %get-tuple-element.2), channel_id=1, replica_groups=mesh['mem'=4,'lat'=2,'lon'=4] {'mem','lat','lon'}, use_global_device_ids=true, to_apply=%region_2.3 | all-reduce | flops 2 | bytes 16 | tf_op jit(solution)/shard_map/psum | solution.py:40
  476.8 1.1 multiply_reduce_fusion.3
  477.9 41.6 %psum.45 = f32[]{:T(128)} all-reduce(f32[]{:T(128)} %multiply_reduce_fusion.3), channel_id=1, replica_groups=mesh['mem'=4,'lat'=2,'lon'=4] {'mem','lat','lon'}, use_global_device_ids=true, to_apply=%region_9.10 | all-reduce | flops 1 | bytes 8 | tf_op jit(solution)/shard_map/psum | solution.py:40
  521.2 1.2 copy-done.6
  522.4 0.8 copy-done.11
  523.2 11.4 %multiply_reduce_fusion = f32[4,96,1536]{2,1,0:T(8,128)} fusion(f32[2,4,96,1536]{3,2,1,0:T(8,128)} %reshape.141, f32[256,1536]{1,0:T(8,128)S(1)} %copy-done.11, f32[256,1536]{1,0:T(8,128)S(1)} %copy-done.9, f32[2,4,96,512]{3,2,1,0:T(8,128)S(1)} %multiply_add_fusion.2, f32[4,512]{1,0:T(4,128)S(1)} %fusion.65), kind=kOutput, calls=%fused_computation.8 | convolution fusion | flops 7251492864 | bytes 11804672 | tf_op jit(solution)/shard_map/dot_general | solution.py:81
  534.6 4.5 copy.54
  539.1 75.7 %all_to_all.92 = f32[4,96,1536]{1,0,2:T(4,128)} all-to-all(f32[4,96,1536]{1,0,2:T(4,128)} %copy.54), channel_id=1, replica_groups=mesh['mem'=4,'lat'=2,'lon'=4] {'lon'}, dimensions={2} | all-to-all | bytes 4718592 | tf_op jit(solution)/shard_map/all_to_all | solution.py:89
  614.8 4.6 copy.56
  619.4 3.2 reshape.137
  622.7 54.8 %all-reduce.6.cloned.1.call-done = f32[589824]{0:T(1024)} async-done(((f32[589824]{0:T(1024)}), f32[589824]{0:T(1024)}) %all-reduce.6.cloned.1.call-update) | async-done | bytes 2359312 | tf_op jit(solution)/shard_map/psum | solution.py:36
  677.4 24.5 %gather_fusion.1 = f32[2048]{0:T(1024)S(1)} fusion(f32[589824]{0:T(1024)} %all-reduce.6.cloned.1.call-done, s32[2048]{0:T(1024)S(1)} %broadcast_clamp_fusion), kind=kCustom, calls=%fused_computation.1 | custom fusion | bytes 24576 | tf_op jit(solution)/shard_map/gather | solution.py:91
  701.9 12.8 %scatter_custom_fusion.2 = f32[589824]{0:T(1024)} fusion(s32[2048]{0:T(1024)S(1)} %bitcast.77, f32[2048]{0:T(1024)S(1)} %mul.240, f32[]{:T(128)} %constant.20.clone.1), kind=kCustom, calls=%fused_computation.71 | custom fusion | flops 2048 | bytes 2359300 | tf_op jit(solution)/shard_map/scatter-add | solution.py:53
  714.7 3.4 reshape.138
  718.1 3.2 copy.57
  721.3 58.4 %all_to_all.93 = f32[4,384,384]{2,0,1:T(4,128)S(1)} all-to-all(f32[4,384,384]{2,0,1:T(4,128)S(1)} %copy.57), channel_id=1, replica_groups=mesh['mem'=4,'lat'=2,'lon'=4] {'lon'}, dimensions={1} | all-to-all | bytes 4718592 | tf_op jit(solution)/shard_map/all_to_all | solution.py:70
  782.3 9.5 %multiply_reduce_fusion.2 = (f32[]{:T(128)}, f32[2,4,96,512]{3,2,1,0:T(8,128)}) fusion(f32[2,4,96,512]{3,2,1,0:T(8,128)S(1)} %copy-done.7, f32[4,512]{1,0:T(4,128)S(1)} %fusion.65, f32[1536,256]{1,0:T(8,128)S(1)} %copy-done.5, f32[1536,256]{1,0:T(8,128)S(1)} %copy-done.3, f32[2,4,96,1536]{3,2,1,0:T(8,128)S(1)} %bitcast.61, f32[4,96,1536]{2,1,0:T(8,128)S(1)} %bitcast.64), kind=kOutput, calls=%fused_computation.39 | convolution fusion | flops 7252082688 | bytes 13377540 | tf_op jit(solution)/shard_map/dot_general | solution.py:57
  791.8 38.3 %psum.47 = f32[]{:T(128)} all-reduce(f32[]{:T(128)} %get-tuple-element.9), channel_id=1, replica_groups=mesh['mem'=4,'lat'=2,'lon'=4] {'mem','lat','lon'}, use_global_device_ids=true, to_apply=%region_14.15 | all-reduce | flops 1 | bytes 8 | tf_op jit(solution)/shard_map/psum | solution.py:93
  831.4 4.3 multiply_subtract_fusion
  (56 shorter events, 6.8 us)
Async XLA Ops:
  29.4 60.3 %all-to-all-start.1 = ((f32[4,384,384]{2,0,1:T(4,128)}), f32[4,384,384]{2,0,1:T(4,128)}, u32[]{:S(2)}, u32[]{:S(2)}) async-start(f32[4,384,384]{2,0,1:T(4,128)} %copy.45), calls=%async_computation.1 | async-start | bytes 4718592 | tf_op jit(solution)/shard_map/all_to_all | solution.py:70
  40.6 53.8 %copy-start.13 = (s32[4]{0:T(128)S(1)}, s32[4]{0:T(128)}, u32[]{:S(2)}) copy-start(s32[4]{0:T(128)} %param.11) | copy-start | bytes 52
  89.6 57.9 %all-to-all-start = ((bf16[2,4,384,384]{3,1,0,2:T(4,128)(2,1)}), bf16[2,4,384,384]{3,1,0,2:T(4,128)(2,1)}, u32[]{:S(2)}, u32[]{:S(2)}) async-start(bf16[2,4,384,384]{3,1,0,2:T(4,128)(2,1)} %copy.43), calls=%async_computation | async-start | bytes 4718592 | tf_op jit(solution)/shard_map/all_to_all | solution.py:67
  94.1 229.7 %all-reduce.4.cloned.1.call-start = ((), (), s32[]{:S(2)}) async-start(), calls=%async_computation.6 | async-start | bytes 4718592 | tf_op jit(solution)/shard_map/psum | solution.py:36
  100.4 59.2 %copy-start.1 = (f32[1536,256]{1,0:T(8,128)}, f32[1536,256]{1,0:T(8,128)S(1)}, u32[]{:S(2)}) copy-start(f32[1536,256]{1,0:T(8,128)S(1)} %fusion.18) | copy-start | bytes 4718596
  159.6 10.9 %copy-start = (f32[2,4,96,1536]{3,2,1,0:T(8,128)S(1)}, f32[2,4,96,1536]{3,2,1,0:T(8,128)}, u32[]{:S(2)}) copy-start(f32[2,4,96,1536]{3,2,1,0:T(8,128)} %reshape.141) | copy-start | bytes 14155780
  159.6 10.9 %copy-start.8 = (f32[256,1536]{1,0:T(8,128)S(1)}, f32[256,1536]{1,0:T(8,128)}, u32[]{:S(2)}) copy-start(f32[256,1536]{1,0:T(8,128)} %fusion.24) | copy-start | bytes 4718596
  159.6 11.0 %copy-start.10 = (f32[256,1536]{1,0:T(8,128)S(1)}, f32[256,1536]{1,0:T(8,128)}, u32[]{:S(2)}) copy-start(f32[256,1536]{1,0:T(8,128)} %fusion.27) | copy-start | bytes 4718596
  268.9 408.5 %all-reduce.6.cloned.1.call-start = ((), (), s32[]{:S(2)}) async-start(), calls=%async_computation.7 | async-start | bytes 4718592 | tf_op jit(solution)/shard_map/psum | solution.py:36
  268.9 79.3 %copy-start.12 = (f32[1,2048]{1,0:T(1,128)S(1)}, f32[1,2048]{1,0:T(1,128)}, u32[]{:S(2)}) copy-start(f32[1,2048]{1,0:T(1,128)} %param.8) | copy-start | bytes 24580
  367.7 59.2 %slice-start = ((s8[4718592]{0:T(1024)(128)(4,1)}), s8[4194304]{0:T(1024)(128)(4,1)S(1)}, s32[]{:S(2)}) async-start(s8[4718592]{0:T(1024)(128)(4,1)} %bitcast.58), calls=%async_computation.8 | async-start | bytes 8388608
  426.4 1.0 slice-start.1
  426.6 1.4 copy-start.2
  426.6 1.9 copy-start.4
  520.8 1.6 copy-start.9
  520.8 2.4 copy-start.11
  521.2 1.2 copy-start.6
  721.3 59.0 %slice-start.2 = ((s8[4718592]{0:T(1024)(128)(4,1)}), s8[4194304]{0:T(1024)(128)(4,1)S(1)}, s32[]{:S(2)}) async-start(s8[4718592]{0:T(1024)(128)(4,1)} %bitcast.60), calls=%async_computation.10 | async-start | bytes 8388608
  779.7 1.0 slice-start.3
  779.9 1.4 copy-start.3
  779.9 1.9 copy-start.5
  779.9 2.4 copy-start.7
Sparse Core Ops, SparseCore 0:
  269.0 54.7 all-reduce.3
  622.8 54.5 all-reduce.5
where the time goes:
time: 851 us; the launch traced here: 843 us
  blocking collectives  387 us (45%)
  waiting for transfers between devices  180 us (21%)
  local copies, waits for them, and re-layouts  122 us (14%)
  other arithmetic  73.6 us (9%)
  matrix products  50.7 us (6%)
  between operations  18.6 us (2%)
  starting transfers between devices  11.1 us (1%)
    all_to_all x2, blocking collectives, body(): lax.all_to_all(partial_value, 'lon', split_axis=2, concat_axis=1, tiled=T...  151 us
    all_to_all x2, blocking collectives, adjoint_part(): lax.all_to_all(gridded, 'lon', split_axis=1, concat_axis=2, tiled=True)  117 us
    psum x2, waiting for transfers between devices, member_total(): return lax.psum(partial_value, 'mem')  110 us
    psum x2, blocking collectives, norm_total(): return lax.psum(jnp.sum(residual * residual), ('mem', 'lat', 'lon'))  79.9 us
    all_to_all x1, waiting for transfers between devices, adjoint_part(): lax.all_to_all(gridded, 'lon', split_axis=1, concat_axis=2, tiled=True)  49 us
    gather x2, local copies, waits for them, and re-layouts, body(): sampled = increment.reshape(-1)[located]  49 us
    scatter-add x3, other arithmetic, gridded_of(): jnp.zeros((levels * tile_rows * tile_cols,), jnp.float32).at[located]  38.4 us
    psum x1, blocking collectives, body(): curvature = lax.psum(jnp.sum(direction * image), ('mem', 'lat', 'lon'))  38.3 us
  transfers between devices with their start and end apart: 4, of which 4 were waited for; matrix products, arithmetic and copies ran while one was open for 4% of the time, Pallas kernels for 0%

commit v1 on v0

--- a/solution.py
+++ b/solution.py
@@ -6,6 +6,12 @@
 NLON = 1536
 KMAX = 256
 ITERS = 2
+
+
+def summed_here(x, axis):
+    parts = lax.all_gather(x, axis, axis=0, tiled=False)
+    summed = parts.sum(axis=0)
+    return summed
 
 
 def basis_table(transposed):
@@ -33,7 +39,7 @@
 
 
 def member_total(partial_value):
-    return lax.psum(partial_value, "mem")
+    return summed_here(partial_value, "mem")
 
 
 def norm_total(residual):

time: 851 us -> 881 us (1.035)
  waiting for transfers between devices: 180 us -> 197 us
  other arithmetic: 73.6 us -> 85.5 us
    all_gather x0 -> x2, waiting for transfers between devices: none -> 127 us  [summed_here(): parts = lax.all_gather(x, axis, axis=0, tiled=False)]
    psum x2 -> x0, waiting for transfers between devices: 110 us -> none  [member_total(): return lax.psum(partial_value, 'mem')]
    reduce_sum x0 -> x2, other arithmetic: none -> 11.9 us  [summed_here(): summed = parts.sum(axis=0)]
where the time goes in v1:
time: 881 us; the launch traced here: 873 us
  blocking collectives  388 us (44%)
  waiting for transfers between devices  197 us (22%)
  local copies, waits for them, and re-layouts  122 us (14%)
  other arithmetic  85.5 us (10%)
  matrix products  50.7 us (6%)
  between operations  18.6 us (2%)
  starting transfers between devices  11.1 us (1%)
    all_to_all x2, blocking collectives, body(): lax.all_to_all(partial_value, 'lon', split_axis=2, concat_axis=1, tiled=T...  151 us
    all_gather x2, waiting for transfers between devices, summed_here(): parts = lax.all_gather(x, axis, axis=0, tiled=False)  127 us
    all_to_all x2, blocking collectives, adjoint_part(): lax.all_to_all(gridded, 'lon', split_axis=1, concat_axis=2, tiled=True)  118 us
    psum x2, blocking collectives, norm_total(): return lax.psum(jnp.sum(residual * residual), ('mem', 'lat', 'lon'))  79.9 us
    all_to_all x1, waiting for transfers between devices, adjoint_part(): lax.all_to_all(gridded, 'lon', split_axis=1, concat_axis=2, tiled=True)  49 us
    gather x2, local copies, waits for them, and re-layouts, body(): sampled = increment.reshape(-1)[located]  49 us
    scatter-add x3, other arithmetic, gridded_of(): jnp.zeros((levels * tile_rows * tile_cols,), jnp.float32).at[located]  38.4 us
    psum x1, blocking collectives, body(): curvature = lax.psum(jnp.sum(direction * image), ('mem', 'lat', 'lon'))  38.1 us
  transfers between devices with their start and end apart: 4, of which 4 were waited for; matrix products, arithmetic and copies ran while one was open for 4% of the time, Pallas kernels for 0%

profile of v1, /device:TPU:0, one launch (start us, length us, event | category | flops | bytes accessed | tf_op | source)
XLA Modules:
  0.0 873.0 jit_solution(2636380998650151632)
XLA Ops:
  8.6 12.8 %scatter_custom_fusion = f32[589824]{0:T(1024)} fusion(s32[2048]{0:T(1024)S(1)} %bitcast.74, f32[2048]{0:T(1024)S(1)} %mul.200, f32[]{:T(128)} %constant.20.clone.1), kind=kCustom, calls=%fused_computation.75 | custom fusion | flops 2048 | bytes 2359300 | tf_op jit(solution)/shard_map/scatter-add | solution.py:59
  21.4 3.4 reshape.136
  24.8 4.6 copy.45
  29.4 6.3 all-to-all-start.1
  35.7 4.9 copy.43
  40.6 49.0 %all-to-all-done.1 = f32[4,384,384]{2,0,1:T(4,128)} async-done(((f32[4,384,384]{2,0,1:T(4,128)}), f32[4,384,384]{2,0,1:T(4,128)}, u32[]{:S(2)}, u32[]{:S(2)}) %all-to-all-start.1) | async-done | bytes 2359328 | tf_op jit(solution)/shard_map/all_to_all | solution.py:76
  89.6 4.5 all-to-all-start
  94.5 5.9 fusion.18
  100.4 8.1 fusion.24
  108.5 6.8 fusion.21
  115.3 7.0 fusion.27
  122.3 1.8 copy.46
  124.2 1.8 copy.66
  125.9 21.6 %all-to-all-done = bf16[2,4,384,384]{3,1,0,2:T(4,128)(2,1)} async-done(((bf16[2,4,384,384]{3,1,0,2:T(4,128)(2,1)}), bf16[2,4,384,384]{3,1,0,2:T(4,128)(2,1)}, u32[]{:S(2)}, u32[]{:S(2)}) %all-to-all-start) | async-done | bytes 2359328 | tf_op jit(solution)/shard_map/all_to_all | solution.py:73
  147.6 5.7 copy.70
  153.3 6.4 reshape.141
  159.6 10.9 %fusion.47 = f32[2,4,96,512]{3,2,1,0:T(8,128)S(1)} fusion(f32[1536,256]{1,0:T(8,128)} %fusion.21, f32[1536,256]{1,0:T(8,128)S(1)} %fusion.18, f32[2,4,96,1536]{3,2,1,0:T(8,128)} %reshape.141, f32[4,96,1536]{2,1,0:T(8,128)} %bitcast.61, f32[4,512]{1,0:T(4,128)S(1)} %fusion.65), kind=kOutput, calls=%fused_computation.70 | convolution fusion | flops 7250903040 | bytes 11804672 | tf_op jit(solution)/shard_map/dot_general | solution.py:63
  170.6 10.3 %multiply_reduce_fusion.1 = f32[4,96,1536]{2,1,0:T(8,128)} fusion(f32[2,4,96,1536]{3,2,1,0:T(8,128)S(1)} %copy-done, f32[256,1536]{1,0:T(8,128)S(1)} %copy-done.10, f32[256,1536]{1,0:T(8,128)S(1)} %copy-done.8, f32[2,4,96,512]{3,2,1,0:T(8,128)S(1)} %fusion.47, f32[4,512]{1,0:T(4,128)S(1)} %fusion.65), kind=kOutput, calls=%fused_computation.11 | convolution fusion | flops 7251492864 | bytes 11804672 | tf_op jit(solution)/shard_map/dot_general | solution.py:87
  180.9 4.5 copy.48
  185.4 75.5 %all_to_all.84 = f32[4,96,1536]{1,0,2:T(4,128)} all-to-all(f32[4,96,1536]{1,0,2:T(4,128)} %copy.48), channel_id=1, replica_groups=mesh['mem'=4,'lat'=2,'lon'=4] {'lon'}, dimensions={2} | all-to-all | bytes 4718592 | tf_op jit(solution)/shard_map/all_to_all | solution.py:95
  261.0 4.7 copy.50
  265.7 63.4 %all-gather.3.cloned.1.call-done = f32[4,4,384,384]{3,2,1,0:T(8,128)} async-done(((f32[1,4,384,384]{3,2,1,0:T(8,128)}), f32[4,4,384,384]{3,2,1,0:T(8,128)}) %all-gather.3.cloned.1.call-update) | async-done | bytes 9437200 | tf_op jit(solution)/shard_map/all_gather | solution.py:12
  329.1 5.9 reduce_sum.74
  335.1 3.2 reshape.137
  338.3 24.5 %gather_fusion = f32[2048]{0:T(1024)S(1)} fusion(f32[589824]{0:T(1024)} %reshape.137, s32[2048]{0:T(1024)S(1)} %broadcast_clamp_fusion), kind=kCustom, calls=%fused_computation | custom fusion | bytes 24576 | tf_op jit(solution)/shard_map/gather | solution.py:97
  362.8 12.8 %scatter_custom_fusion.1 = f32[589824]{0:T(1024)} fusion(s32[2048]{0:T(1024)S(1)} %bitcast.76, f32[2048]{0:T(1024)S(1)} %mul.226, f32[]{:T(128)} %constant.20.clone.1), kind=kCustom, calls=%fused_computation.73 | custom fusion | flops 2048 | bytes 2359300 | tf_op jit(solution)/shard_map/scatter-add | solution.py:59
  375.6 3.4 reshape.138
  379.0 3.2 copy.51
  382.2 59.3 %all_to_all.85 = f32[4,384,384]{2,0,1:T(4,128)S(1)} all-to-all(f32[4,384,384]{2,0,1:T(4,128)S(1)} %copy.51), channel_id=1, replica_groups=mesh['mem'=4,'lat'=2,'lon'=4] {'lon'}, dimensions={1} | all-to-all | bytes 4718592 | tf_op jit(solution)/shard_map/all_to_all | solution.py:76
  443.7 8.6 multiply_reduce_fusion.4
  452.2 38.1 %all-reduce = (f32[]{:T(128)}, f32[]{:T(128)}) all-reduce(f32[]{:T(128)} %get-tuple-element.3, f32[]{:T(128)} %get-tuple-element.2), channel_id=1, replica_groups=mesh['mem'=4,'lat'=2,'lon'=4] {'mem','lat','lon'}, use_global_device_ids=true, to_apply=%region_2.3 | all-reduce | flops 2 | bytes 16 | tf_op jit(solution)/shard_map/psum | solution.py:46
  492.8 41.8 %psum.30 = f32[]{:T(128)} all-reduce(f32[]{:T(128)} %multiply_reduce_fusion.3), channel_id=1, replica_groups=mesh['mem'=4,'lat'=2,'lon'=4] {'mem','lat','lon'}, use_global_device_ids=true, to_apply=%region_9.10 | all-reduce | flops 1 | bytes 8 | tf_op jit(solution)/shard_map/psum | solution.py:46
  536.4 1.2 copy-done.6
  538.4 11.4 %multiply_reduce_fusion = f32[4,96,1536]{2,1,0:T(8,128)} fusion(f32[2,4,96,1536]{3,2,1,0:T(8,128)} %reshape.141, f32[256,1536]{1,0:T(8,128)S(1)} %copy-done.11, f32[256,1536]{1,0:T(8,128)S(1)} %copy-done.9, f32[2,4,96,512]{3,2,1,0:T(8,128)S(1)} %multiply_add_fusion.2, f32[4,512]{1,0:T(4,128)S(1)} %fusion.65), kind=kOutput, calls=%fused_computation.8 | convolution fusion | flops 7251492864 | bytes 11804672 | tf_op jit(solution)/shard_map/dot_general | solution.py:87
  549.8 4.5 copy.54
  554.3 75.7 %all_to_all.86 = f32[4,96,1536]{1,0,2:T(4,128)} all-to-all(f32[4,96,1536]{1,0,2:T(4,128)} %copy.54), channel_id=1, replica_groups=mesh['mem'=4,'lat'=2,'lon'=4] {'lon'}, dimensions={2} | all-to-all | bytes 4718592 | tf_op jit(solution)/shard_map/all_to_all | solution.py:95
  630.0 4.6 copy.56
  634.6 63.3 %all-gather.5.cloned.1.call-done = f32[4,4,384,384]{3,2,1,0:T(8,128)} async-done(((f32[1,4,384,384]{3,2,1,0:T(8,128)}), f32[4,4,384,384]{3,2,1,0:T(8,128)}) %all-gather.5.cloned.1.call-update) | async-done | bytes 9437200 | tf_op jit(solution)/shard_map/all_gather | solution.py:12
  697.9 6.0 reduce_sum.78
  703.9 3.2 reshape.139
  707.1 24.5 %gather_fusion.1 = f32[2048]{0:T(1024)S(1)} fusion(f32[589824]{0:T(1024)} %reshape.139, s32[2048]{0:T(1024)S(1)} %broadcast_clamp_fusion), kind=kCustom, calls=%fused_computation.1 | custom fusion | bytes 24576 | tf_op jit(solution)/shard_map/gather | solution.py:97
  731.6 12.8 %scatter_custom_fusion.2 = f32[589824]{0:T(1024)} fusion(s32[2048]{0:T(1024)S(1)} %bitcast.77, f32[2048]{0:T(1024)S(1)} %mul.240, f32[]{:T(128)} %constant.20.clone.1), kind=kCustom, calls=%fused_computation.71 | custom fusion | flops 2048 | bytes 2359300 | tf_op jit(solution)/shard_map/scatter-add | solution.py:59
  744.4 3.4 reshape.140
  747.8 3.2 copy.57
  751.0 59.1 %all_to_all.87 = f32[4,384,384]{2,0,1:T(4,128)S(1)} all-to-all(f32[4,384,384]{2,0,1:T(4,128)S(1)} %copy.57), channel_id=1, replica_groups=mesh['mem'=4,'lat'=2,'lon'=4] {'lon'}, dimensions={1} | all-to-all | bytes 4718592 | tf_op jit(solution)/shard_map/all_to_all | solution.py:76
  812.7 9.5 %multiply_reduce_fusion.2 = (f32[]{:T(128)}, f32[2,4,96,512]{3,2,1,0:T(8,128)}) fusion(f32[2,4,96,512]{3,2,1,0:T(8,128)S(1)} %copy-done.7, f32[4,512]{1,0:T(4,128)S(1)} %fusion.65, f32[1536,256]{1,0:T(8,128)S(1)} %copy-done.5, f32[1536,256]{1,0:T(8,128)S(1)} %copy-done.3, f32[2,4,96,1536]{3,2,1,0:T(8,128)S(1)} %bitcast.59, f32[4,96,1536]{2,1,0:T(8,128)S(1)} %bitcast.62), kind=kOutput, calls=%fused_computation.39 | convolution fusion | flops 7252082688 | bytes 13377540 | tf_op jit(solution)/shard_map/dot_general | solution.py:63
  822.2 38.1 %psum.31 = f32[]{:T(128)} all-reduce(f32[]{:T(128)} %get-tuple-element.9), channel_id=1, replica_groups=mesh['mem'=4,'lat'=2,'lon'=4] {'mem','lat','lon'}, use_global_device_ids=true, to_apply=%region_14.15 | all-reduce | flops 1 | bytes 8 | tf_op jit(solution)/shard_map/psum | solution.py:99
  861.6 4.3 multiply_subtract_fusion
  (58 shorter events, 8.8 us)
Async XLA Ops:
  29.4 60.3 %all-to-all-start.1 = ((f32[4,384,384]{2,0,1:T(4,128)}), f32[4,384,384]{2,0,1:T(4,128)}, u32[]{:S(2)}, u32[]{:S(2)}) async-start(f32[4,384,384]{2,0,1:T(4,128)} %copy.45), calls=%async_computation.1 | async-start | bytes 4718592 | tf_op jit(solution)/shard_map/all_to_all | solution.py:76
  40.6 53.8 %copy-start.13 = (s32[4]{0:T(128)S(1)}, s32[4]{0:T(128)}, u32[]{:S(2)}) copy-start(s32[4]{0:T(128)} %param.11) | copy-start | bytes 52
  89.6 57.9 %all-to-all-start = ((bf16[2,4,384,384]{3,1,0,2:T(4,128)(2,1)}), bf16[2,4,384,384]{3,1,0,2:T(4,128)(2,1)}, u32[]{:S(2)}, u32[]{:S(2)}) async-start(bf16[2,4,384,384]{3,1,0,2:T(4,128)(2,1)} %copy.43), calls=%async_computation | async-start | bytes 4718592 | tf_op jit(solution)/shard_map/all_to_all | solution.py:73
  94.1 235.0 %all-gather.3.cloned.1.call-start = ((), (), s32[]{:S(2)}) async-start(), calls=%async_computation.6 | async-start | bytes 11796480 | tf_op jit(solution)/shard_map/all_gather | solution.py:12
  100.4 59.2 %copy-start.1 = (f32[1536,256]{1,0:T(8,128)}, f32[1536,256]{1,0:T(8,128)S(1)}, u32[]{:S(2)}) copy-start(f32[1536,256]{1,0:T(8,128)S(1)} %fusion.18) | copy-start | bytes 4718596
  159.6 10.9 %copy-start = (f32[2,4,96,1536]{3,2,1,0:T(8,128)S(1)}, f32[2,4,96,1536]{3,2,1,0:T(8,128)}, u32[]{:S(2)}) copy-start(f32[2,4,96,1536]{3,2,1,0:T(8,128)} %reshape.141) | copy-start | bytes 14155780
  159.6 10.9 %copy-start.8 = (f32[256,1536]{1,0:T(8,128)S(1)}, f32[256,1536]{1,0:T(8,128)}, u32[]{:S(2)}) copy-start(f32[256,1536]{1,0:T(8,128)} %fusion.24) | copy-start | bytes 4718596
  159.6 11.0 %copy-start.10 = (f32[256,1536]{1,0:T(8,128)S(1)}, f32[256,1536]{1,0:T(8,128)}, u32[]{:S(2)}) copy-start(f32[256,1536]{1,0:T(8,128)} %fusion.27) | copy-start | bytes 4718596
  265.7 432.3 %all-gather.5.cloned.1.call-start = ((), (), s32[]{:S(2)}) async-start(), calls=%async_computation.7 | async-start | bytes 11796480 | tf_op jit(solution)/shard_map/all_gather | solution.py:12
  338.3 24.5 %copy-start.12 = (f32[1,2048]{1,0:T(1,128)S(1)}, f32[1,2048]{1,0:T(1,128)}, u32[]{:S(2)}) copy-start(f32[1,2048]{1,0:T(1,128)} %param.8) | copy-start | bytes 24580
  382.2 59.9 %slice-start = ((s8[4718592]{0:T(1024)(128)(4,1)}), s8[4194304]{0:T(1024)(128)(4,1)S(1)}, s32[]{:S(2)}) async-start(s8[4718592]{0:T(1024)(128)(4,1)} %bitcast.56), calls=%async_computation.8 | async-start | bytes 8388608
  441.6 1.0 slice-start.1
  441.7 1.4 copy-start.2
  441.8 1.9 copy-start.4
  536.0 1.6 copy-start.9
  536.0 2.4 copy-start.11
  536.4 1.2 copy-start.6
  751.0 59.6 %slice-start.2 = ((s8[4718592]{0:T(1024)(128)(4,1)}), s8[4194304]{0:T(1024)(128)(4,1)S(1)}, s32[]{:S(2)}) async-start(s8[4718592]{0:T(1024)(128)(4,1)} %bitcast.58), calls=%async_computation.10 | async-start | bytes 8388608
  810.1 1.0 slice-start.3
  810.3 1.4 copy-start.3
  810.3 1.9 copy-start.5
  810.3 2.4 copy-start.7
Sparse Core Ops, SparseCore 0:
  265.8 63.3 all-gather.2
  634.7 63.1 all-gather.4
